TPU v7x, 32 devices: a whole 2x2x4 slice. The times are simulated.
32 devices in a mesh: ent: 8 (over z, y), rep: 4 (over x, core).
Axes of the slice: x: 2, y: 2, z: 4, core: 2. Of those that a mesh axis runs over, the one named last changes fastest.
Arguments:
- facts: bfloat16 [65536, 512], P(('ent', 'rep')), may hold values from -6 to 6
- fact_owner: int32 [65536, 1], P(('ent', 'rep')), may hold values from 0 to 7; in each aligned block of 2048 rows (0 to 2047, 2048 to 4095, ...) at most 512 rows name the same one
- fact_slot: int32 [65536], P(('ent', 'rep')), may hold values from 0 to 127
- entity_feats: bfloat16 [1024, 512], P('ent'), may hold values from -6 to 6
- out_cotangent: bfloat16 [1024, 512], P('ent'), may hold values from -6 to 6
- w_msg: bfloat16 [512, 512], replicated, may hold values from -0.25 to 0.25
- w_upd: bfloat16 [512, 512], replicated, may hold values from -0.25 to 0.25
Outputs:
- ent_out: bfloat16 [1024, 512], P('ent')
- fact_grad: bfloat16 [65536, 512], P(('ent', 'rep'))
- msg_weight_grad: float32 [512, 512], P(('ent', 'rep'))
- upd_weight_grad_t: float32 [512, 512], P(('ent', 'rep'))
Inputs may be any that keep to these rules, and one draw needn't show every extreme that they name: `fact_owner`: among the rows of one device, at most 512 name the same owner.
All inputs are finite; a program needn't handle non-finite values.
Results may differ from a plain program's by a relative error of at most 0.0065.
Values may be sent and summed in bfloat16 or wider, within the bound.
A program may use at most 64 MiB of HBM per device.

v0:
```python
import jax
import jax.numpy as jnp
from jax import lax
from jax.sharding import PartitionSpec as P


def silu_grad(value):
    sig = jax.nn.sigmoid(value)
    return sig * (1.0 + value * (1.0 - sig))


def per_device(facts, fact_owner, fact_slot, entity_feats, out_cotangent, w_msg, w_upd):
    n_owners = lax.axis_size("ent")
    n_copies = lax.axis_size("rep")
    fact_rows, width = facts.shape
    ent_rows = entity_feats.shape[0]
    capacity = 2 * fact_rows // n_owners
    owner = fact_owner[:, 0]
    hits = (owner[:, None] == jnp.arange(n_owners, dtype=jnp.int32)[None, :]).astype(jnp.int32)
    placed = jnp.sum(jnp.cumsum(hits, axis=0) * hits, axis=1) - 1
    slot_buf = jnp.full((n_owners, capacity), -1, jnp.int32).at[owner, placed].set(fact_slot)
    recv_slots = lax.all_to_all(slot_buf, "ent", split_axis=0, concat_axis=0, tiled=True)
    flat_slots = recv_slots.reshape(n_owners * capacity)
    onehot = (jnp.arange(ent_rows, dtype=jnp.int32)[:, None] == flat_slots[None, :]).astype(
        jnp.bfloat16
    )
    pre = jnp.dot(facts, w_msg, preferred_element_type=jnp.float32)
    message = jax.nn.silu(pre).astype(jnp.bfloat16)
    send_buf = jnp.zeros((n_owners, capacity, width), jnp.bfloat16).at[owner, placed].set(message)
    received = lax.all_to_all(send_buf, "ent", split_axis=0, concat_axis=0, tiled=True)
    flat = received.reshape(n_owners * capacity, width)
    part_agg = jnp.dot(onehot, flat, preferred_element_type=jnp.float32)
    part_count = jnp.sum(onehot, axis=1, dtype=jnp.float32)
    agg, count = lax.psum((part_agg, part_count), "rep")
    denom = jnp.maximum(count, 1.0)[:, None]
    mean = (agg / denom).astype(jnp.bfloat16)
    zval = jnp.dot(mean, w_upd, preferred_element_type=jnp.float32)
    ent_out = (entity_feats.astype(jnp.float32) + jax.nn.silu(zval)).astype(jnp.bfloat16)
    grad_z = (out_cotangent.astype(jnp.float32) * silu_grad(zval)).astype(jnp.bfloat16)
    d_mean = lax.dot_general(
        grad_z, w_upd, (((1,), (1,)), ((), ())), preferred_element_type=jnp.float32
    )
    d_agg = (d_mean / denom).astype(jnp.bfloat16)
    spread = lax.dot_general(
        onehot, d_agg, (((0,), (0,)), ((), ())), preferred_element_type=jnp.float32
    )
    back_buf = spread.astype(jnp.bfloat16).reshape(n_owners, capacity, width)
    returned = lax.all_to_all(back_buf, "ent", split_axis=0, concat_axis=0, tiled=True)
    d_msg = returned[owner, placed]
    d_pre = (d_msg.astype(jnp.float32) * silu_grad(pre)).astype(jnp.bfloat16)
    fact_grad = lax.dot_general(
        d_pre, w_msg, (((1,), (1,)), ((), ())), preferred_element_type=jnp.float32
    ).astype(jnp.bfloat16)
    share = ent_rows // n_copies
    begin = lax.axis_index("rep") * share
    grad_part = lax.dynamic_slice_in_dim(grad_z, begin, share, 0)
    mean_part = lax.dynamic_slice_in_dim(mean, begin, share, 0)
    left = lax.dot_general(
        facts, d_pre, (((0,), (0,)), ((), ())), preferred_element_type=jnp.float32
    )
    right = lax.dot_general(
        grad_part, mean_part, (((0,), (0,)), ((), ())), preferred_element_type=jnp.float32
    )
    grads = lax.psum_scatter(
        jnp.concatenate([left, right], axis=1), ("ent", "rep"), scatter_dimension=0, tiled=True
    )
    return (ent_out, fact_grad, grads[:, :width], grads[:, width:])


def solution(mesh):
    placed = (
        P(("ent", "rep"), None),
        P(("ent", "rep"), None),
        P(("ent", "rep")),
        P("ent", None),
        P("ent", None),
        P(),
        P(),
    )
    return jax.shard_map(
        per_device,
        mesh=mesh,
        in_specs=placed,
        out_specs=(
            P("ent", None),
            P(("ent", "rep"), None),
            P(("ent", "rep"), None),
            P(("ent", "rep"), None),
        ),
        check_vma=False,
    )
```

profile of v0, /device:TPU:0, one launch (start us, length us, event | category | flops | bytes accessed | tf_op | source)
XLA Modules:
  0.0 475.2 jit_solution(11818568556852053850)
XLA Ops:
  8.0 2.3 reduce-window.6
  13.9 8.8 %scatter_custom_fusion = s32[4096]{0:T(1024)} fusion(s32[2048]{0:T(1024)S(1)} %broadcast_select_fusion, s32[2048]{0:T(1024)} %param.9, s32[]{:T(128)} %constant.10.clone.1), kind=kCustom, calls=%fused_computation.43 | custom fusion | bytes 16896
  22.7 7.3 %all-to-all-start = ((s32[8,1,512]{2,1,0:T(1,128)}), s32[8,1,512]{2,1,0:T(1,128)S(1)}, u32[]{:S(2)}, u32[]{:S(2)}) async-start(s32[8,1,512]{2,1,0:T(1,128)} %bitcast.5), calls=%async_computation | async-start | bytes 32768 | tf_op jit(solution)/shard_map/all_to_all | solution.py:22
  29.9 4.2 fusion.19
  34.2 13.6 %scatter_custom_fusion.1 = bf16[4096,512]{1,0:T(8,128)(2,1)} fusion(s32[2048]{0:T(1024)S(1)} %broadcast_select_fusion, f32[2048,512]{1,0:T(8,128)} %fusion.19, bf16[]{:T(256)} %constant.14.clone.1, f32[]{:T(128)} %constant.15.clone.1), kind=kCustom, calls=%fused_computation.8 | custom fusion | flops 5242880 | bytes 8388614
  47.8 6.0 %all-to-all-start.1 = ((bf16[8,512,512]{2,1,0:T(8,128)(2,1)}), bf16[8,512,512]{2,1,0:T(8,128)(2,1)}, u32[]{:S(2)}, u32[]{:S(2)}) async-start(bf16[8,512,512]{2,1,0:T(8,128)(2,1)} %bitcast.41), calls=%async_computation.1 | async-start | bytes 8388608 | tf_op jit(solution)/shard_map/all_to_all | solution.py:30
  54.1 5.7 %psum.15 = f32[128]{0:T(128)S(1)} all-reduce(f32[128]{0:T(128)S(1)} %convert_reduce_fusion), channel_id=1, replica_groups=mesh['ent'=8,'rep'=4] {'rep'}, use_global_device_ids=true, to_apply=%region_7.8 | all-reduce | flops 128 | bytes 1024 | tf_op jit(solution)/shard_map/psum | solution.py:34
  59.9 86.6 %all-to-all-done.1 = bf16[8,512,512]{2,1,0:T(8,128)(2,1)} async-done(((bf16[8,512,512]{2,1,0:T(8,128)(2,1)}), bf16[8,512,512]{2,1,0:T(8,128)(2,1)}, u32[]{:S(2)}, u32[]{:S(2)}) %all-to-all-start.1) | async-done | bytes 4194336 | tf_op jit(solution)/shard_map/all_to_all | solution.py:30
  146.5 3.7 fusion.4
  150.2 31.2 %all-reduce.2.cloned.1.call-done = f32[128,512]{1,0:T(8,128)} async-done(((f32[128,512]{1,0:T(8,128)}), f32[128,512]{1,0:T(8,128)}) %all-reduce.2.cloned.1.call-update) | async-done | bytes 262160 | tf_op jit(solution)/shard_map/psum | solution.py:34
  181.4 1.0 divide_convert_fusion
  182.5 1.0 multiply_convert_fusion.3
  183.5 3.5 convolution_convert_fusion
  187.0 5.5 %all-to-all-start.2 = ((bf16[8,512,512]{2,1,0:T(8,128)(2,1)}), bf16[8,512,512]{2,1,0:T(8,128)(2,1)}, u32[]{:S(2)}, u32[]{:S(2)}) async-start(bf16[8,512,512]{2,1,0:T(8,128)(2,1)} %bitcast.40), calls=%async_computation.2 | async-start | bytes 8388608 | tf_op jit(solution)/shard_map/all_to_all | solution.py:48
  193.1 91.6 %all-to-all-done.2 = bf16[8,512,512]{2,1,0:T(8,128)(2,1)} async-done(((bf16[8,512,512]{2,1,0:T(8,128)(2,1)}), bf16[8,512,512]{2,1,0:T(8,128)(2,1)}, u32[]{:S(2)}, u32[]{:S(2)}) %all-to-all-start.2) | async-done | bytes 4194336 | tf_op jit(solution)/shard_map/all_to_all | solution.py:48
  284.7 37.2 %gather_fusion = bf16[2048,512]{1,0:T(8,128)(2,1)} fusion(bf16[8,512,512]{2,1,0:T(8,128)(2,1)} %all-to-all-done.2, s32[2048]{0:T(1024)S(1)} %bitcast.39), kind=kCustom, calls=%fused_computation | custom fusion | bytes 4210688 | tf_op jit(solution)/shard_map/gather | solution.py:49
  321.9 4.5 multiply_convert_fusion
  326.4 1.3 convolution_bitcast_fusion
  327.7 1.5 pad_maximum_fusion
  329.2 2.9 copy.19
  332.1 1.0 copy-done.3
  333.1 4.2 convolution_convert_fusion.1
  337.3 129.6 %reduce-scatter.4.cloned.1.call-done = f32[16,1024]{1,0:T(8,128)} async-done(((f32[512,1024]{1,0:T(8,128)}), f32[16,1024]{1,0:T(8,128)}) %reduce-scatter.4.cloned.1.call-update) | async-done | bytes 65552
  466.9 1.4 fusion.18
  (29 shorter events, 5.4 us)
Async XLA Ops:
  7.2 22.8 %copy-start = (bf16[2048,512]{1,0:T(8,128)(2,1)S(1)}, bf16[2048,512]{1,0:T(8,128)(2,1)}, u32[]{:S(2)}) copy-start(bf16[2048,512]{1,0:T(8,128)(2,1)} %param.7) | copy-start | bytes 6291460
  22.7 25.1 %all-to-all-start = ((s32[8,1,512]{2,1,0:T(1,128)}), s32[8,1,512]{2,1,0:T(1,128)S(1)}, u32[]{:S(2)}, u32[]{:S(2)}) async-start(s32[8,1,512]{2,1,0:T(1,128)} %bitcast.5), calls=%async_computation | async-start | bytes 32768 | tf_op jit(solution)/shard_map/all_to_all | solution.py:22
  47.8 98.7 %all-to-all-start.1 = ((bf16[8,512,512]{2,1,0:T(8,128)(2,1)}), bf16[8,512,512]{2,1,0:T(8,128)(2,1)}, u32[]{:S(2)}, u32[]{:S(2)}) async-start(bf16[8,512,512]{2,1,0:T(8,128)(2,1)} %bitcast.41), calls=%async_computation.1 | async-start | bytes 8388608 | tf_op jit(solution)/shard_map/all_to_all | solution.py:30
  53.8 127.6 %all-reduce.2.cloned.1.call-start = ((), (), s32[]{:S(2)}) async-start(), calls=%async_computation.4 | async-start | bytes 524288 | tf_op jit(solution)/shard_map/psum | solution.py:34
  146.5 35.9 %copy-start.2 = (bf16[512,512]{1,0:T(8,128)(2,1)S(1)}, bf16[512,512]{1,0:T(8,128)(2,1)}, u32[]{:S(2)}) copy-start(bf16[512,512]{1,0:T(8,128)(2,1)} %param.13) | copy-start | bytes 1572868
  146.5 35.9 %copy-start.4 = (bf16[128,512]{1,0:T(8,128)(2,1)S(1)}, bf16[128,512]{1,0:T(8,128)(2,1)}, u32[]{:S(2)}) copy-start(bf16[128,512]{1,0:T(8,128)(2,1)} %param.11) | copy-start | bytes 393220
  146.5 35.9 %copy-start.5 = (bf16[128,512]{1,0:T(8,128)(2,1)S(1)}, bf16[128,512]{1,0:T(8,128)(2,1)}, u32[]{:S(2)}) copy-start(bf16[128,512]{1,0:T(8,128)(2,1)} %param.10) | copy-start | bytes 393220
  187.0 97.7 %all-to-all-start.2 = ((bf16[8,512,512]{2,1,0:T(8,128)(2,1)}), bf16[8,512,512]{2,1,0:T(8,128)(2,1)}, u32[]{:S(2)}, u32[]{:S(2)}) async-start(bf16[8,512,512]{2,1,0:T(8,128)(2,1)} %bitcast.40), calls=%async_computation.2 | async-start | bytes 8388608 | tf_op jit(solution)/shard_map/all_to_all | solution.py:48
  192.5 274.4 %reduce-scatter.4.cloned.1.call-start = ((), (), s32[]{:S(2)}) async-start(), calls=%async_computation.5 | async-start | bytes 2162688
  326.4 1.4 copy-start.1
  332.1 1.0 copy-start.3
Sparse Core Ops, SparseCore 0:
  150.4 31.0 all-reduce.1
  332.2 134.6 reduce-scatter.3
where the time goes:
time: 477 us; the launch traced here: 475 us
  waiting for transfers between devices  339 us (71%)
  local copies, waits for them, and re-layouts  51.7 us (11%)
  other arithmetic  27.3 us (6%)
  starting transfers between devices  19 us (4%)
  matrix products  18.2 us (4%)
  between operations  14.2 us (3%)
  blocking collectives  5.73 us (1%)
    unnamed x3, waiting for transfers between devices  130 us
    all_to_all x1, waiting for transfers between devices, per_device(): lax.all_to_all(back_buf, 'ent', split_axis=0, concat_axis=0, tiled=True)  91.6 us
    all_to_all x1, waiting for transfers between devices, per_device(): lax.all_to_all(send_buf, 'ent', split_axis=0, concat_axis=0, tiled=True)  86.6 us
    gather x1, local copies, waits for them, and re-layouts, per_device(): d_msg = returned[owner, placed]  37.2 us
    psum x1, waiting for transfers between devices, per_device(): agg, count = lax.psum((part_agg, part_count), 'rep')  31.2 us
    unnamed x5, other arithmetic  15.2 us
    unnamed x14, local copies, waits for them, and re-layouts  12.8 us
  transfers between devices with their start and end apart: 5, of which 4 were waited for; matrix products, arithmetic and copies ran while one was open for 5% of the time, Pallas kernels for 0%

commit v1 on v0

v1 whole, which is shorter than its diff:
```python
import jax
import jax.numpy as jnp
from jax import lax
from jax.sharding import PartitionSpec as P


def silu_grad(value):
    sig = jax.nn.sigmoid(value)
    return sig * (1.0 + value * (1.0 - sig))


def per_device(facts, fact_owner, fact_slot, entity_feats, out_cotangent, w_msg, w_upd):
    n_owners = lax.axis_size("ent")
    n_copies = lax.axis_size("rep")
    width = facts.shape[1]
    ent_rows = entity_feats.shape[0]
    ents = ent_rows * n_owners
    share = ent_rows // n_copies
    key = fact_owner[:, 0] * ent_rows + fact_slot
    onehot = (jnp.arange(ents, dtype=jnp.int32)[:, None] == key[None, :]).astype(jnp.bfloat16)
    pre = jnp.dot(facts, w_msg, preferred_element_type=jnp.float32)
    message = jax.nn.silu(pre).astype(jnp.bfloat16)
    part_agg = jnp.dot(onehot, message, preferred_element_type=jnp.float32)
    part_count = jnp.sum(onehot, axis=1, dtype=jnp.float32)
    part = jnp.concatenate([part_agg, jnp.broadcast_to(part_count[:, None], (ents, 128))], axis=1)
    both = lax.psum_scatter(part, ("ent", "rep"), scatter_dimension=0, tiled=True)
    agg = both[:, :width]
    denom = jnp.maximum(both[:, width:width + 1], 1.0)
    begin = lax.axis_index("rep") * share
    feats = lax.dynamic_slice_in_dim(entity_feats, begin, share, 0)
    cot = lax.dynamic_slice_in_dim(out_cotangent, begin, share, 0)
    mean = (agg / denom).astype(jnp.bfloat16)
    zval = jnp.dot(mean, w_upd, preferred_element_type=jnp.float32)
    ent_part = (feats.astype(jnp.float32) + jax.nn.silu(zval)).astype(jnp.bfloat16)
    grad_z = (cot.astype(jnp.float32) * silu_grad(zval)).astype(jnp.bfloat16)
    d_mean = lax.dot_general(
        grad_z, w_upd, (((1,), (1,)), ((), ())), preferred_element_type=jnp.float32
    )
    d_agg = (d_mean / denom).astype(jnp.bfloat16)
    d_all = lax.all_gather(d_agg, ("ent", "rep"), axis=0, tiled=True)
    ent_out = lax.all_gather(ent_part, "rep", axis=0, tiled=True)
    d_msg = lax.dot_general(
        onehot, d_all, (((0,), (0,)), ((), ())), preferred_element_type=jnp.float32
    )
    d_pre = (d_msg * silu_grad(pre)).astype(jnp.bfloat16)
    fact_grad = lax.dot_general(
        d_pre, w_msg, (((1,), (1,)), ((), ())), preferred_element_type=jnp.float32
    ).astype(jnp.bfloat16)
    left = lax.dot_general(
        facts, d_pre, (((0,), (0,)), ((), ())), preferred_element_type=jnp.float32
    )
    right = lax.dot_general(
        grad_z, mean, (((0,), (0,)), ((), ())), preferred_element_type=jnp.float32
    )
    grads = lax.psum_scatter(
        jnp.concatenate([left, right], axis=1), ("ent", "rep"), scatter_dimension=0, tiled=True
    )
    return (ent_out, fact_grad, grads[:, :width], grads[:, width:])


def solution(mesh):
    placed = (
        P(("ent", "rep"), None),
        P(("ent", "rep"), None),
        P(("ent", "rep")),
        P("ent", None),
        P("ent", None),
        P(),
        P(),
    )
    return jax.shard_map(
        per_device,
        mesh=mesh,
        in_specs=placed,
        out_specs=(
            P("ent", None),
            P(("ent", "rep"), None),
            P(("ent", "rep"), None),
            P(("ent", "rep"), None),
        ),
        check_vma=False,
    )
```

time: 477 us -> 370 us (0.78)
  local copies, waits for them, and re-layouts: 51.7 us -> 8.47 us
  waiting for transfers between devices: 339 us -> 315 us
  other arithmetic: 27.3 us -> 6.59 us
  starting transfers between devices: 19 us -> 0.12 us
    all_to_all x3 -> x0, waiting for transfers between devices: 178 us -> none  [the longest x1 91.6 us: per_device(): lax.all_to_all(back_buf, 'ent', split_axis=0, concat_axis=0, tiled=True)]
    reduce_scatter x0 -> x1, waiting for transfers between devices: none -> 140 us  [per_device(): lax.psum_scatter(part, ('ent', 'rep'), scatter_dimension=0, tiled=True)]
    all_gather x0 -> x1, waiting for transfers between devices: none -> 48.9 us  [per_device(): d_all = lax.all_gather(d_agg, ('ent', 'rep'), axis=0, tiled=True)]
    gather x1 -> x0, local copies, waits for them, and re-layouts: 37.2 us -> none  [per_device(): d_msg = returned[owner, placed]]
    psum x1 -> x0, waiting for transfers between devices: 31.2 us -> none  [per_device(): agg, count = lax.psum((part_agg, part_count), 'rep')]
    all_to_all x3 -> x0, starting transfers between devices: 18.8 us -> none  [the longest x1 7.28 us: per_device(): lax.all_to_all(slot_buf, 'ent', split_axis=0, concat_axis=0, tiled=True)]
    unnamed x5 -> x0, other arithmetic: 15.2 us -> none
    convert_element_type x3 -> x0, other arithmetic: 6.35 us -> none  [the longest x1 4.46 us: per_device(): d_pre = (d_msg.astype(jnp.float32) * silu_grad(pre)).astype(jnp.bfloat16)]
  transfers between devices with their start and end apart: 5 -> 3, of which waited for: 4 -> 3; matrix products, arithmetic and copies ran while one was open for 5% -> 1% of each run, Pallas kernels for 0% -> 0%
where the time goes in v1:
time: 370 us; the launch traced here: 369 us
  waiting for transfers between devices  315 us (85%)
  matrix products  19.9 us (5%)
  between operations  13.8 us (4%)
  local copies, waits for them, and re-layouts  8.47 us (2%)
  other arithmetic  6.59 us (2%)
  blocking collectives  5.43 us (1%)
    reduce_scatter x1, waiting for transfers between devices, per_device(): lax.psum_scatter(part, ('ent', 'rep'), scatter_dimension=0, tiled=True)  140 us
    unnamed x4, waiting for transfers between devices  126 us
    all_gather x1, waiting for transfers between devices, per_device(): d_all = lax.all_gather(d_agg, ('ent', 'rep'), axis=0, tiled=True)  48.9 us
  transfers between devices with their start and end apart: 3, of which 3 were waited for; matrix products, arithmetic and copies ran while one was open for 1% of the time, Pallas kernels for 0%

profile of v1, /device:TPU:0, one launch (start us, length us, event | category | flops | bytes accessed | tf_op | source)
XLA Modules:
  0.0 369.4 jit_solution(3396001357918936834)
XLA Ops:
  7.2 0.8 broadcast_multiply_fusion
  8.1 0.7 add.31
  8.8 0.9 convert_reduce_fusion
  9.7 2.3 fusion.13
  12.0 2.8 fusion.2
  14.9 1.9 pad_maximum_fusion
  16.8 3.3 copy.19
  20.2 140.3 %reduce-scatter.7.cloned.1.call-done = f32[32,640]{1,0:T(8,128)} async-done(((f32[1024,640]{1,0:T(8,128)}), f32[32,640]{1,0:T(8,128)}) %reduce-scatter.7.cloned.1.call-update) | async-done | bytes 81936 | tf_op jit(solution)/shard_map/reduce_scatter | solution.py:26
  160.5 0.7 slice_maximum_fusion
  161.2 0.1 copy.26
  161.3 1.1 add_convert_fusion
  162.4 0.9 fusion.5
  163.4 1.3 fusion.8
  164.6 48.9 %all-gather.2.cloned.1.call-done = bf16[1024,512]{1,0:T(8,128)(2,1)} async-done(((bf16[32,512]{1,0:T(8,128)(2,1)}), bf16[1024,512]{1,0:T(8,128)(2,1)}) %all-gather.2.cloned.1.call-update) | async-done | bytes 1048592 | tf_op jit(solution)/shard_map/all_gather | solution.py:40
  213.5 6.1 %multiply_convert_fusion = bf16[2048,512]{1,0:T(8,128)(2,1)S(1)} fusion(f32[2048,512]{1,0:T(8,128)} %copy-done.1, bf16[1024,512]{1,0:T(8,128)(2,1)} %all-gather.2.cloned.1.call-done, s32[2048]{0:T(1024)S(1)} %add.31), kind=kOutput, calls=%fused_computation.5 | convolution fusion | flops 2159017984 | bytes 7348224 | tf_op jit(solution)/shard_map/dot_general | solution.py:42
  219.6 1.3 convolution_bitcast_fusion
  220.9 0.0 copy-done.5
  221.0 1.5 pad_maximum_fusion.1
  222.4 2.9 copy.21
  225.4 5.4 %all_gather.6 = bf16[128,512]{1,0:T(8,128)(2,1)S(1)} all-gather(bf16[32,512]{1,0:T(8,128)(2,1)S(1)} %get-tuple-element.18), channel_id=1, replica_groups=mesh['ent'=8,'rep'=4] {'rep'}, dimensions={0}, use_global_device_ids=true | all-gather | bytes 163840 | tf_op jit(solution)/shard_map/all_gather | solution.py:41
  230.8 4.2 %convolution_convert_fusion = bf16[2048,512]{1,0:T(8,128)(2,1)} fusion(bf16[2048,512]{1,0:T(8,128)(2,1)} %copy-done.5, bf16[512,512]{1,0:T(8,128)(2,1)S(1)} %copy-done.2), kind=kOutput, calls=%fused_computation.10 | convolution fusion | flops 1074790400 | bytes 4718592 | tf_op jit(solution)/shard_map/dot_general | solution.py:46
  235.0 125.8 %reduce-scatter.9.cloned.1.call-done = f32[16,1024]{1,0:T(8,128)} async-done(((f32[512,1024]{1,0:T(8,128)}), f32[16,1024]{1,0:T(8,128)}) %reduce-scatter.9.cloned.1.call-update) | async-done | bytes 65552
  360.8 1.4 fusion.12
  362.2 0.7 copy.28
  (18 shorter events, 0.2 us)
Async XLA Ops:
  7.2 2.5 copy-start
  7.2 153.3 %reduce-scatter.7.cloned.1.call-start = ((), (), s32[]{:S(2)}) async-start(), calls=%async_computation.3 | async-start | bytes 2703360 | tf_op jit(solution)/shard_map/reduce_scatter | solution.py:26
  12.0 2.8 copy-start.1
  20.1 141.2 %copy-start.4 = (bf16[512,512]{1,0:T(8,128)(2,1)S(1)}, bf16[512,512]{1,0:T(8,128)(2,1)}, u32[]{:S(2)}) copy-start(bf16[512,512]{1,0:T(8,128)(2,1)} %param.13) | copy-start | bytes 1572868
  20.1 142.3 %copy-start.3 = (bf16[128,512]{1,0:T(8,128)(2,1)S(1)}, bf16[128,512]{1,0:T(8,128)(2,1)}, u32[]{:S(2)}) copy-start(bf16[128,512]{1,0:T(8,128)(2,1)} %param.11) | copy-start | bytes 393220
  20.1 193.4 %all-gather.2.cloned.1.call-start = ((), (), s32[]{:S(2)}) async-start(), calls=%async_computation.2 | async-start | bytes 1081344 | tf_op jit(solution)/shard_map/all_gather | solution.py:40
  163.3 197.5 %reduce-scatter.9.cloned.1.call-start = ((), (), s32[]{:S(2)}) async-start(), calls=%async_computation.4 | async-start | bytes 2162688
  219.6 1.3 copy-start.5
  222.4 8.4 %copy-start.2 = (bf16[512,512]{1,0:T(8,128)(2,1)S(1)}, bf16[512,512]{1,0:T(8,128)(2,1)}, u32[]{:S(2)}) copy-start(bf16[512,512]{1,0:T(8,128)(2,1)} %param.12) | copy-start | bytes 1572868
Sparse Core Ops, SparseCore 0:
  20.2 140.2 reduce-scatter.6
  163.9 49.5 all-gather.1
  225.5 135.2 reduce-scatter.8

commit v2 on v1

v2 whole, which is shorter than its diff:
```python
import functools

import jax
import jax.numpy as jnp
from jax import lax
from jax.experimental import pallas as pl
from jax.experimental.pallas import tpu as pltpu
from jax.sharding import PartitionSpec as P

E_HI, E_LO, R_HI, R_LO = range(4)
ORDER_A = (R_LO, R_HI, E_LO, E_HI)
ORDER_B = (R_LO, E_LO, R_HI, E_HI)
MESH = pl.DeviceIdType.MESH
VMEM_LIMIT = 56 << 20


def silu_grad(value):
    sig = jax.nn.sigmoid(value)
    return sig * (1.0 + value * (1.0 - sig))


def position():
    ent, rep = lax.axis_index("ent"), lax.axis_index("rep")
    return (ent // 2, lax.rem(ent, 2), rep // 2, lax.rem(rep, 2))


def device_at(here, dim, coord):
    if dim == E_HI:
        return {"ent": coord * 2 + here[E_LO]}
    if dim == E_LO:
        return {"ent": here[E_HI] * 2 + coord}
    if dim == R_HI:
        return {"rep": coord * 2 + here[R_LO]}
    return {"rep": here[R_HI] * 2 + coord}


def enter(grid, here):
    barrier = pltpu.get_barrier_semaphore()
    rep = here[R_HI] * 2 + here[R_LO]
    n_rep = grid[R_HI] * grid[R_LO]
    total = 0
    for step in range(1, n_rep):
        pl.semaphore_signal(
            barrier, inc=1, device_id={"rep": lax.rem(rep + step, n_rep)}, device_id_type=MESH
        )
        total += 1
    for dim in (E_HI, E_LO):
        for step in range(1, grid[dim]):
            target = device_at(here, dim, lax.rem(here[dim] + step, grid[dim]))
            pl.semaphore_signal(barrier, inc=1, device_id=target, device_id_type=MESH)
            total += 1
    pl.semaphore_wait(barrier, total)


def sum_scratch(grid, order, tail, dtype):
    left, shapes = [0, 1, 2, 3], []
    for dim in order:
        left.remove(dim)
        kept = tuple(grid[d] for d in left) + tail
        final = not left
        shapes += [
            pltpu.VMEM((grid[dim] - 1,) + kept, dtype),
            pltpu.VMEM(kept, jnp.float32 if final else dtype),
            pltpu.SemaphoreType.DMA((grid[dim] - 1,)),
            pltpu.SemaphoreType.DMA((grid[dim] - 1,)),
        ]
    return shapes


class Scatter:
    def __init__(self, grid, here, order, source, scratch):
        self.grid, self.here, self.order, self.current = grid, here, order, source
        self.scratch, self.left, self.stage = scratch, [0, 1, 2, 3], 0

    def start(self):
        dim = self.order[self.stage]
        size, mine = self.grid[dim], self.here[dim]
        arrived, _, send, recv = self.scratch[4 * self.stage:4 * self.stage + 4]
        lead = (slice(None),) * self.left.index(dim)
        self.copies = []
        for step in range(1, size):
            coord = lax.rem(mine + step, size)
            copy = pltpu.make_async_remote_copy(
                src_ref=self.current.at[lead + (coord,)],
                dst_ref=arrived.at[step - 1],
                send_sem=send.at[step - 1],
                recv_sem=recv.at[step - 1],
                device_id=device_at(self.here, dim, coord),
                device_id_type=MESH,
            )
            copy.start()
            self.copies.append(copy)

    def finish(self):
        dim = self.order[self.stage]
        arrived, total, _, _ = self.scratch[4 * self.stage:4 * self.stage + 4]
        lead = (slice(None),) * self.left.index(dim)
        value = self.current[lead + (self.here[dim],)].astype(jnp.float32)
        for index, copy in enumerate(self.copies):
            copy.wait()
            value = value + arrived[index].astype(jnp.float32)
        total[...] = value.astype(total.dtype)
        self.current = total
        self.left.remove(dim)
        self.stage += 1


class Gather:
    def __init__(self, grid, here, order, columns, ref, sems):
        self.grid, self.here, self.order = grid, here, order
        self.columns, self.ref, self.sems = columns, ref, sems
        self.done, self.stage = [], 0

    def start(self):
        dim = self.order[self.stage]
        size, mine = self.grid[dim], self.here[dim]
        send, recv = self.sems[2 * self.stage:2 * self.stage + 2]
        index = tuple(slice(None) if d in self.done else self.here[d] for d in range(4))
        block = self.ref.at[index + (slice(None), self.columns)]
        self.copies = []
        for step in range(1, size):
            coord = lax.rem(mine + step, size)
            copy = pltpu.make_async_remote_copy(
                src_ref=block,
                dst_ref=block,
                send_sem=send.at[step - 1],
                recv_sem=recv.at[step - 1],
                device_id=device_at(self.here, dim, coord),
                device_id_type=MESH,
            )
            copy.start()
            self.copies.append(copy)

    def finish(self):
        for copy in self.copies:
            copy.wait()
        self.done.append(self.order[self.stage])
        self.stage += 1


def gather_scratch(grid, order):
    return [pltpu.SemaphoreType.DMA((grid[d] - 1,)) for d in order for _ in range(2)]


def entity_kernel(grid, part_ref, count_ref, feats_ref, cot_ref, w_ref,
                  all_ref, ent_ref, mean_ref, gz_ref, *scratch):
    here = position()
    rep = lax.axis_index("rep")
    n_rep = grid[R_HI] * grid[R_LO]
    half = part_ref.shape[-1] // 2
    share = part_ref.shape[-2]
    enter(grid, here)
    every = (slice(None),) * 5
    sums = [
        Scatter(grid, here, ORDER_A, count_ref, scratch[0:16]),
        Scatter(grid, here, ORDER_A, part_ref.at[every + (slice(0, half),)], scratch[16:32]),
        Scatter(grid, here, ORDER_B, part_ref.at[every + (slice(half, 2 * half),)], scratch[32:48]),
    ]
    for item in sums:
        item.start()
    for stage in range(4):
        for item in sums:
            item.finish()
            if stage < 3:
                item.start()
    lane = lax.broadcasted_iota(jnp.int32, (share, 128), 1)
    row = lax.broadcasted_iota(jnp.int32, (share, 128), 0)
    counts = jnp.broadcast_to(sums[0].current[0:1, :], (share, 128))
    count = jnp.sum(jnp.where(lane == row, counts, 0.0), axis=1, keepdims=True)
    denom = jnp.maximum(count, 1.0)
    agg = jnp.concatenate([sums[1].current[...], sums[2].current[...]], axis=1)
    mean = (agg / denom).astype(jnp.bfloat16)
    zval = jnp.dot(mean, w_ref[...], preferred_element_type=jnp.float32)
    grad_z = (cot_ref[rep].astype(jnp.float32) * silu_grad(zval)).astype(jnp.bfloat16)
    d_mean = lax.dot_general(
        grad_z, w_ref[...], (((1,), (1,)), ((), ())), preferred_element_type=jnp.float32
    )
    all_ref[here] = (d_mean / denom).astype(jnp.bfloat16)
    spreads = [
        Gather(grid, here, ORDER_A[::-1], slice(0, half), all_ref, scratch[48:56]),
        Gather(grid, here, ORDER_B[::-1], slice(half, 2 * half), all_ref, scratch[56:64]),
    ]
    for item in spreads:
        item.start()
    mean_ref[...] = mean
    gz_ref[...] = grad_z
    ent_ref[rep] = (feats_ref[rep].astype(jnp.float32) + zval * jax.nn.sigmoid(zval)).astype(
        jnp.bfloat16
    )
    ent_copies = []
    for step in range(1, n_rep):
        copy = pltpu.make_async_remote_copy(
            src_ref=ent_ref.at[rep],
            dst_ref=ent_ref.at[rep],
            send_sem=scratch[64].at[step - 1],
            recv_sem=scratch[65].at[step - 1],
            device_id={"rep": lax.rem(rep + step, n_rep)},
            device_id_type=MESH,
        )
        copy.start()
        ent_copies.append(copy)
    for stage in range(4):
        for item in spreads:
            item.finish()
            if stage < 3:
                item.start()
    for copy in ent_copies:
        copy.wait()


def grads_kernel(grid, left_ref, right_ref, d_pre_ref, w_ref, msg_ref, upd_ref, fact_ref, *scratch):
    here = position()
    enter(grid, here)
    sums = [
        Scatter(grid, here, ORDER_A, left_ref, scratch[0:16]),
        Scatter(grid, here, ORDER_B, right_ref, scratch[16:32]),
    ]
    for item in sums:
        item.start()
    rows = d_pre_ref.shape[0] // 4
    for stage in range(4):
        part = pl.ds(stage * rows, rows)
        fact_ref[part, :] = lax.dot_general(
            d_pre_ref[part, :], w_ref[...], (((1,), (1,)), ((), ())),
            preferred_element_type=jnp.float32,
        ).astype(jnp.bfloat16)
        for item in sums:
            item.finish()
            if stage < 3:
                item.start()
    msg_ref[...] = sums[0].current[...]
    upd_ref[...] = sums[1].current[...]


def in_vmem(number):
    return [pl.BlockSpec(memory_space=pltpu.VMEM)] * number


def per_device(facts, fact_owner, fact_slot, entity_feats, out_cotangent, w_msg, w_upd):
    n_owners = lax.axis_size("ent")
    n_copies = lax.axis_size("rep")
    grid = (n_owners // 2, 2, n_copies // 2, 2)
    fact_rows, width = facts.shape
    ent_rows = entity_feats.shape[0]
    ents = ent_rows * n_owners
    share = ent_rows // n_copies
    bf16, f32 = jnp.bfloat16, jnp.float32
    key = fact_owner[:, 0] * ent_rows + fact_slot
    onehot = (jnp.arange(ents, dtype=jnp.int32)[:, None] == key[None, :]).astype(bf16)
    pre = jnp.dot(facts, w_msg, preferred_element_type=f32)
    message = jax.nn.silu(pre).astype(bf16)
    part = jnp.dot(onehot, message, preferred_element_type=f32).astype(bf16)
    count = jnp.sum(onehot, axis=1, dtype=f32).reshape(grid + (1, share))
    count = jnp.broadcast_to(jnp.pad(count, ((0, 0),) * 5 + ((0, 128 - share),)), grid + (8, 128))
    rep_sem = pltpu.SemaphoreType.DMA((n_copies - 1,))
    d_all, ent_out, mean, grad_z = pl.pallas_call(
        functools.partial(entity_kernel, grid),
        out_shape=(
            jax.ShapeDtypeStruct(grid + (share, width), bf16),
            jax.ShapeDtypeStruct((n_copies, share, width), bf16),
            jax.ShapeDtypeStruct((share, width), bf16),
            jax.ShapeDtypeStruct((share, width), bf16),
        ),
        in_specs=in_vmem(5),
        out_specs=in_vmem(4),
        scratch_shapes=(
            sum_scratch(grid, ORDER_A, (8, 128), f32)
            + sum_scratch(grid, ORDER_A, (share, width // 2), bf16)
            + sum_scratch(grid, ORDER_B, (share, width // 2), bf16)
            + gather_scratch(grid, ORDER_A[::-1])
            + gather_scratch(grid, ORDER_B[::-1])
            + [rep_sem, rep_sem]
        ),
        compiler_params=pltpu.CompilerParams(
            collective_id=0, has_side_effects=True, vmem_limit_bytes=VMEM_LIMIT
        ),
    )(
        part.reshape(grid + (share, width)),
        count,
        entity_feats.reshape(n_copies, share, width),
        out_cotangent.reshape(n_copies, share, width),
        w_upd,
    )
    d_msg = lax.dot_general(
        onehot, d_all.reshape(ents, width), (((0,), (0,)), ((), ())), preferred_element_type=f32
    )
    d_pre = (d_msg * silu_grad(pre)).astype(bf16)
    left = lax.dot_general(
        facts, d_pre, (((0,), (0,)), ((), ())), preferred_element_type=f32
    ).astype(bf16)
    right = lax.dot_general(
        grad_z, mean, (((0,), (0,)), ((), ())), preferred_element_type=f32
    ).astype(bf16)
    rows = width // (n_owners * n_copies)
    msg_grad, upd_grad, fact_grad = pl.pallas_call(
        functools.partial(grads_kernel, grid),
        out_shape=(
            jax.ShapeDtypeStruct((rows, width), f32),
            jax.ShapeDtypeStruct((rows, width), f32),
            jax.ShapeDtypeStruct((fact_rows, width), bf16),
        ),
        in_specs=in_vmem(4),
        out_specs=in_vmem(3),
        scratch_shapes=(
            sum_scratch(grid, ORDER_A, (rows, width), bf16)
            + sum_scratch(grid, ORDER_B, (rows, width), bf16)
        ),
        compiler_params=pltpu.CompilerParams(
            collective_id=1, has_side_effects=True, vmem_limit_bytes=VMEM_LIMIT
        ),
    )(left.reshape(grid + (rows, width)), right.reshape(grid + (rows, width)), d_pre, w_msg)
    return (ent_out.reshape(ent_rows, width), fact_grad, msg_grad, upd_grad)


def solution(mesh):
    placed = (
        P(("ent", "rep"), None),
        P(("ent", "rep"), None),
        P(("ent", "rep")),
        P("ent", None),
        P("ent", None),
        P(),
        P(),
    )
    return jax.shard_map(
        per_device,
        mesh=mesh,
        in_specs=placed,
        out_specs=(
            P("ent", None),
            P(("ent", "rep"), None),
            P(("ent", "rep"), None),
            P(("ent", "rep"), None),
        ),
        check_vma=False,
    )
```

time: 370 us -> 80.7 us (0.22)
  waiting for transfers between devices: 315 us -> 0 us
  Pallas kernels: 0 us -> 56.4 us
  between operations: 13.8 us -> 0.72 us
  matrix products: 19.9 us -> 13.7 us
  blocking collectives: 5.43 us -> 0 us
  other arithmetic: 6.59 us -> 2.46 us
    reduce_scatter x1 -> x0, waiting for transfers between devices: 140 us -> none  [per_device(): lax.psum_scatter(part, ('ent', 'rep'), scatter_dimension=0, tiled=True)]
    unnamed x4 -> x0, waiting for transfers between devices: 126 us -> none
    pallas_call x0 -> x2, Pallas kernels: none -> 56.4 us  [the longest x1 36.8 us: per_device(): pl.pallas_call(functools.partial(entity_kernel, grid), out_shape=(jax.Sha...]
    all_gather x1 -> x0, waiting for transfers between devices: 48.9 us -> none  [per_device(): d_all = lax.all_gather(d_agg, ('ent', 'rep'), axis=0, tiled=True)]
    dot_general x6 -> x3, matrix products: 17.4 us -> 10.5 us  [the longest x1 4.78 us: per_device(): lax.dot_general(onehot, d_all.reshape(ents, width), (((0,), (0,)), ((), (...]
    all_gather x1 -> x0, blocking collectives: 5.43 us -> none  [per_device(): ent_out = lax.all_gather(ent_part, 'rep', axis=0, tiled=True)]
  transfers between devices with their start and end apart: 3 -> 0, of which waited for: 3 -> 0; matrix products, arithmetic and copies ran while one was open for 1% -> 0% of each run, Pallas kernels for 0% -> 0%
where the time goes in v2:
time: 80.7 us; the launch traced here: 80.4 us
  Pallas kernels  56.4 us (70%)
  matrix products  13.7 us (17%)
  local copies, waits for them, and re-layouts  7.03 us (9%)
  other arithmetic  2.46 us (3%)
    pallas_call x1, Pallas kernels, per_device(): pl.pallas_call(functools.partial(entity_kernel, grid), out_shape=(jax.Sha...  36.8 us
    pallas_call x1, Pallas kernels, per_device(): pl.pallas_call(functools.partial(grads_kernel, grid), out_shape=(jax.Shap...  19.6 us
    unnamed x18, local copies, waits for them, and re-layouts  6.27 us
    dot_general x1, matrix products, per_device(): lax.dot_general(onehot, d_all.reshape(ents, width), (((0,), (0,)), ((), (...  4.78 us
    dot_general x1, matrix products, per_device(): part = jnp.dot(onehot, message, preferred_element_type=f32).astype(bf16)  3.41 us
    dot_general x1, matrix products, per_device(): pre = jnp.dot(facts, w_msg, preferred_element_type=f32)  2.29 us
    dot_general x1, matrix products, per_device(): lax.dot_general(facts, d_pre, (((0,), (0,)), ((), ())), preferred_element...  2.12 us

profile of v2, /device:TPU:0, one launch (start us, length us, event | category | flops | bytes accessed | tf_op | source)
XLA Modules:
  0.0 80.4 jit_solution(16189699152498590781)
XLA Ops:
  0.6 0.0 copy-start
  0.6 0.9 %broadcast_multiply_fusion = s32[2048,1]{0,1:T(1,128)S(1)} fusion(s32[2048,1]{0,1:T(1,128)} %param.8), kind=kLoop, calls=%fused_computation.14 | loop fusion | flops 2048 | bytes 16384 | tf_op jit(solution)/shard_map/mul | solution.py:248
  1.5 0.7 add.13
  2.2 0.9 %convert_reduce_fusion = f32[1024]{0:T(1024)S(1)} fusion(s32[2048]{0:T(1024)S(1)} %add.13), kind=kLoop, calls=%fused_computation | loop fusion | flops 8387584 | bytes 12288 | tf_op jit(solution)/shard_map/reduce_sum | solution.py:253
  3.1 0.1 reshape.36
  3.2 0.7 broadcast_in_dim.10.count_ref
  3.9 0.0 copy-done
  3.9 2.3 %fusion.7 = f32[2048,512]{1,0:T(8,128)S(1)} fusion(bf16[2048,512]{1,0:T(8,128)(2,1)S(1)} %copy-done, bf16[512,512]{1,0:T(8,128)(2,1)} %w_ref.3), kind=kOutput, calls=%fused_computation.16 | convolution fusion | flops 1073741824 | bytes 6815744 | tf_op jit(solution)/shard_map/dot_general | solution.py:250
  6.2 3.4 %fusion.5 = bf16[1024,512]{1,0:T(8,128)(2,1)} fusion(f32[2048,512]{1,0:T(8,128)S(1)} %fusion.7, s32[2048]{0:T(1024)S(1)} %add.13), kind=kOutput, calls=%fused_computation.10 | convolution fusion | flops 2155347968 | bytes 5251072 | tf_op jit(solution)/shard_map/dot_general | solution.py:252
  9.6 36.8 %shard_map.102 = (bf16[4,2,2,2,32,512]{5,4,3,2,1,0:T(8,128)(2,1)}, bf16[4,32,512]{2,1,0:T(8,128)(2,1)}, bf16[32,512]{1,0:T(8,128)(2,1)}, bf16[32,512]{1,0:T(8,128)(2,1)}) custom-call(bf16[4,2,2,2,32,512]{5,4,3,2,1,0:T(8,128)(2,1)} %bitcast.20, f32[4,2,2,2,8,128]{5,4,3,2,1,0:T(8,128)} %broadcast_in_dim.10.count_ref, bf16[4,32,512]{2,1,0:T(8,128)(2,1)} %bitcast.23, ...), custom_call_target="tpu_custom_call" | custom-call | tf_op jit(solution)/shard_map/pallas_call | solution.py:256
  46.4 4.8 %multiply_convert_fusion.d_pre_ref = bf16[2048,512]{1,0:T(8,128)(2,1)S(1)} fusion(f32[2048,512]{1,0:T(8,128)S(1)} %fusion.7, bf16[1024,512]{1,0:T(8,128)(2,1)} %bitcast.26, s32[2048]{0:T(1024)S(1)} %add.13), kind=kOutput, calls=%fused_computation.5 | convolution fusion | flops 2159017984 | bytes 7348224 | tf_op jit(solution)/shard_map/dot_general | solution.py:284
  51.2 0.0 copy-start.1
  51.2 1.3 %copy-done.1 = bf16[2048,512]{1,0:T(8,128)(2,1)} copy-done((bf16[2048,512]{1,0:T(8,128)(2,1)}, bf16[2048,512]{1,0:T(8,128)(2,1)S(1)}, u32[]{:S(2)}) %copy-start.1) | copy-done | bytes 2097176
  52.5 2.1 %convolution_convert_fusion = bf16[512,512]{0,1:T(8,128)(2,1)} fusion(bf16[2048,512]{1,0:T(8,128)(2,1)S(1)} %multiply_convert_fusion.d_pre_ref, bf16[2048,512]{1,0:T(8,128)(2,1)S(1)} %copy-done), kind=kOutput, calls=%fused_computation.11 | convolution fusion | flops 1074003968 | bytes 4718592 | tf_op jit(solution)/shard_map/dot_general | solution.py:288
  54.6 0.0 copy-done.3
  54.6 0.0 copy-done.4
  54.7 1.1 %convolution_convert_fusion.1 = bf16[512,512]{1,0:T(8,128)(2,1)} fusion(bf16[32,512]{1,0:T(8,128)(2,1)S(1)} %copy-done.4, bf16[32,512]{1,0:T(8,128)(2,1)S(1)} %copy-done.3), kind=kOutput, calls=%fused_computation.12 | convolution fusion | flops 17039360 | bytes 589824 | tf_op jit(solution)/shard_map/dot_general | solution.py:291
  55.8 19.6 %shard_map.103 = (f32[16,512]{1,0:T(8,128)}, f32[16,512]{1,0:T(8,128)}, bf16[2048,512]{1,0:T(8,128)(2,1)}) custom-call(bf16[4,2,2,2,16,512]{5,4,3,2,1,0:T(8,128)(2,1)} %bitcast.21, bf16[4,2,2,2,16,512]{5,4,3,2,1,0:T(8,128)(2,1)} %bitcast.19, bf16[2048,512]{1,0:T(8,128)(2,1)} %copy-done.1, bf16[512,512]{1,0:T(8,128)(2,1)} %w_ref.3), custom_call_target="tpu_custom_call" | custom-call | tf_op jit(solution)/shard_map/pallas_call | solution.py:295
  75.4 0.0 copy-start.6
  75.4 0.7 copy.15
  76.1 3.0 %copy.16 = bf16[2048,512]{1,0:T(8,128)(2,1)} copy(bf16[2048,512]{1,0:T(8,128)(2,1)} %get-tuple-element.23) | data formatting | bytes 4194304
  79.1 0.0 copy-done.6
  79.1 0.6 copy.17
  79.7 0.6 copy.18
  (7 shorter events, 0.0 us)
Async XLA Ops:
  0.6 3.2 %copy-start = (bf16[2048,512]{1,0:T(8,128)(2,1)S(1)}, bf16[2048,512]{1,0:T(8,128)(2,1)}, u32[]{:S(2)}) copy-start(bf16[2048,512]{1,0:T(8,128)(2,1)} %param.7) | copy-start | bytes 6291460
  51.2 1.3 %copy-start.1 = (bf16[2048,512]{1,0:T(8,128)(2,1)}, bf16[2048,512]{1,0:T(8,128)(2,1)S(1)}, u32[]{:S(2)}) copy-start(bf16[2048,512]{1,0:T(8,128)(2,1)S(1)} %multiply_convert_fusion.d_pre_ref) | copy-start | bytes 6291460
  52.5 2.1 %copy-start.3 = (bf16[32,512]{1,0:T(8,128)(2,1)S(1)}, bf16[32,512]{1,0:T(8,128)(2,1)}, u32[]{:S(2)}) copy-start(bf16[32,512]{1,0:T(8,128)(2,1)} %get-tuple-element.14) | copy-start | bytes 98308
  52.5 2.1 %copy-start.4 = (bf16[32,512]{1,0:T(8,128)(2,1)S(1)}, bf16[32,512]{1,0:T(8,128)(2,1)}, u32[]{:S(2)}) copy-start(bf16[32,512]{1,0:T(8,128)(2,1)} %get-tuple-element.13) | copy-start | bytes 98308
  52.5 22.9 %copy-start.2 = (bf16[4,32,512]{2,1,0:T(8,128)(2,1)S(1)}, bf16[4,32,512]{2,1,0:T(8,128)(2,1)}, u32[]{:S(2)}) copy-start(bf16[4,32,512]{2,1,0:T(8,128)(2,1)} %get-tuple-element.11) | copy-start | bytes 393220
  75.4 3.7 %copy-start.6 = (f32[16,512]{1,0:T(8,128)S(1)}, f32[16,512]{1,0:T(8,128)}, u32[]{:S(2)}) copy-start(f32[16,512]{1,0:T(8,128)} %get-tuple-element.24) | copy-start | bytes 98308
  75.4 4.3 %copy-start.5 = (f32[16,512]{1,0:T(8,128)S(1)}, f32[16,512]{1,0:T(8,128)}, u32[]{:S(2)}) copy-start(f32[16,512]{1,0:T(8,128)} %get-tuple-element.25) | copy-start | bytes 98308

commit v3 on v2

v3 whole, which is shorter than its diff:
```python
import functools

import jax
import jax.numpy as jnp
from jax import lax
from jax.experimental import pallas as pl
from jax.experimental.pallas import tpu as pltpu
from jax.sharding import PartitionSpec as P

E_HI, E_LO, R_HI, R_LO = range(4)
ORDER_A = (R_LO, R_HI, E_LO, E_HI)
ORDER_B = (R_LO, E_LO, R_HI, E_HI)
MESH = pl.DeviceIdType.MESH
VMEM_LIMIT = 56 << 20


def silu_grad(value):
    sig = jax.nn.sigmoid(value)
    return sig * (1.0 + value * (1.0 - sig))


def position():
    ent, rep = lax.axis_index("ent"), lax.axis_index("rep")
    return (ent // 2, lax.rem(ent, 2), rep // 2, lax.rem(rep, 2))


def device_at(here, dim, coord):
    if dim == E_HI:
        return {"ent": coord * 2 + here[E_LO]}
    if dim == E_LO:
        return {"ent": here[E_HI] * 2 + coord}
    if dim == R_HI:
        return {"rep": coord * 2 + here[R_LO]}
    return {"rep": here[R_HI] * 2 + coord}


def greet(grid, here):
    barrier = pltpu.get_barrier_semaphore()
    rep = here[R_HI] * 2 + here[R_LO]
    n_rep = grid[R_HI] * grid[R_LO]
    total = 0
    for step in range(1, n_rep):
        pl.semaphore_signal(
            barrier, inc=1, device_id={"rep": lax.rem(rep + step, n_rep)}, device_id_type=MESH
        )
        total += 1
    for dim in (E_HI, E_LO):
        for step in range(1, grid[dim]):
            target = device_at(here, dim, lax.rem(here[dim] + step, grid[dim]))
            pl.semaphore_signal(barrier, inc=1, device_id=target, device_id_type=MESH)
            total += 1
    return total


def sum_scratch(grid, order, tail, dtype):
    left, shapes = [0, 1, 2, 3], []
    for dim in order:
        left.remove(dim)
        kept = tuple(grid[d] for d in left) + tail
        shapes += [
            pltpu.VMEM((grid[dim] - 1,) + kept, dtype),
            pltpu.VMEM(kept, jnp.float32),
            pltpu.VMEM(kept if left else (16, 128), dtype),
            pltpu.SemaphoreType.DMA((grid[dim] - 1,)),
            pltpu.SemaphoreType.DMA((grid[dim] - 1,)),
        ]
    return shapes


class Scatter:
    def __init__(self, grid, here, order, own, sent, scratch):
        self.grid, self.here, self.order, self.own, self.sent = grid, here, order, own, sent
        self.scratch, self.left, self.stage = scratch, [0, 1, 2, 3], 0

    def start(self):
        dim = self.order[self.stage]
        size, mine = self.grid[dim], self.here[dim]
        arrived, _, _, send, recv = self.scratch[5 * self.stage:5 * self.stage + 5]
        lead = (slice(None),) * self.left.index(dim)
        self.copies = []
        for step in range(1, size):
            coord = lax.rem(mine + step, size)
            copy = pltpu.make_async_remote_copy(
                src_ref=self.sent.at[lead + (coord,)],
                dst_ref=arrived.at[step - 1],
                send_sem=send.at[step - 1],
                recv_sem=recv.at[step - 1],
                device_id=device_at(self.here, dim, coord),
                device_id_type=MESH,
            )
            copy.start()
            self.copies.append(copy)

    def finish(self):
        dim = self.order[self.stage]
        arrived, total, rounded, _, _ = self.scratch[5 * self.stage:5 * self.stage + 5]
        lead = (slice(None),) * self.left.index(dim)
        value = self.own[lead + (self.here[dim],)]
        for index, copy in enumerate(self.copies):
            copy.wait()
            value = value + arrived[index].astype(jnp.float32)
        total[...] = value
        self.own = self.sent = total
        self.left.remove(dim)
        self.stage += 1
        if self.left and rounded.dtype != jnp.float32:
            rounded[...] = value.astype(rounded.dtype)
            self.sent = rounded

    def advance(self):
        self.finish()
        if self.stage < 4:
            self.start()


class Gather:
    def __init__(self, grid, here, order, columns, ref, sems):
        self.grid, self.here, self.order = grid, here, order
        self.columns, self.ref, self.sems = columns, ref, sems
        self.done, self.stage = [], 0

    def start(self):
        dim = self.order[self.stage]
        size, mine = self.grid[dim], self.here[dim]
        send, recv = self.sems[2 * self.stage:2 * self.stage + 2]
        index = tuple(slice(None) if d in self.done else self.here[d] for d in range(4))
        block = self.ref.at[index + (slice(None), self.columns)]
        self.copies = []
        for step in range(1, size):
            coord = lax.rem(mine + step, size)
            copy = pltpu.make_async_remote_copy(
                src_ref=block,
                dst_ref=block,
                send_sem=send.at[step - 1],
                recv_sem=recv.at[step - 1],
                device_id=device_at(self.here, dim, coord),
                device_id_type=MESH,
            )
            copy.start()
            self.copies.append(copy)

    def advance(self):
        for copy in self.copies:
            copy.wait()
        self.done.append(self.order[self.stage])
        self.stage += 1
        if self.stage < 4:
            self.start()


def gather_scratch(grid, order):
    return [pltpu.SemaphoreType.DMA((grid[d] - 1,)) for d in order for _ in range(2)]


def layer_kernel(grid, facts_ref, key_ref, feats_ref, cot_ref, w_ref, w_upd_ref,
                 d_pre_ref, ent_ref, grads_ref, *scratch):
    bf16, f32 = jnp.bfloat16, jnp.float32
    here = position()
    rep = lax.axis_index("rep")
    n_rep = grid[R_HI] * grid[R_LO]
    greeted = greet(grid, here)
    scratch = list(scratch)

    def take(number):
        taken, scratch[:number] = scratch[:number], []
        return taken

    gate_ref, part_ref, part_sent, hot_ref, facts_t, all_ref, count_ref = take(7)
    side_ref, side_sent, left_ref, left_sent = take(4)
    message_ref = d_pre_ref
    fact_rows, width = facts_ref.shape
    half = width // 2
    halves = [slice(0, half), slice(half, width)]
    share = part_ref.shape[-2]
    ent_rows = share * n_rep
    block = fact_rows // 4
    pair = 2 * ent_rows
    kept = hot_ref.shape[0] > pair
    every = (slice(None),) * 5
    counts = Scatter(grid, here, ORDER_A, count_ref, count_ref, take(20))
    sums = [
        Scatter(grid, here, order, part_ref.at[every + (cols,)], part_sent.at[every + (cols,)],
                take(20))
        for order, cols in zip((ORDER_A, ORDER_B), halves)
    ]
    spreads = [
        Gather(grid, here, order[::-1], cols, all_ref, take(8))
        for order, cols in zip((ORDER_A, ORDER_B), halves)
    ]
    sides = Scatter(grid, here, ORDER_A, side_ref, side_sent, take(20))
    lefts = [
        Scatter(grid, here, order, left_ref.at[every + (cols,)], left_sent.at[every + (cols,)],
                take(20))
        for order, cols in zip((ORDER_A, ORDER_B), halves)
    ]
    ent_send, ent_recv = take(2)

    for number, cols in enumerate(halves):

        def project(step, carry, cols=cols):
            rows = pl.ds(pl.multiple_of(step * block, block), block)
            pre = jnp.dot(facts_ref[rows, :], w_ref[:, cols], preferred_element_type=f32)
            sig = jax.nn.sigmoid(pre)
            gate_ref[rows, cols] = sig * (1.0 + pre * (1.0 - sig))
            message_ref[rows, cols] = (pre * sig).astype(bf16)
            return carry

        lax.fori_loop(0, 4, project, 0)

        def gather_sums(step, carry, number=number, cols=cols):
            rows = pl.ds(pl.multiple_of(step * pair, pair), pair) if kept else pl.ds(0, pair)
            if number == 0 or not kept:
                ids = lax.broadcasted_iota(jnp.int32, (pair, fact_rows), 0) + step * pair
                hit = (ids == key_ref[...]).astype(f32)
                hot_ref[rows, :] = hit.astype(bf16)
                if number == 0:
                    total = jnp.sum(hit, axis=1, keepdims=True)
                    for low in range(2):
                        column = jnp.broadcast_to(
                            total[low * ent_rows:(low + 1) * ent_rows], (ent_rows, 128)
                        )
                        line = jnp.transpose(column)[0:8, :]
                        count_ref[step, low] = jnp.broadcast_to(
                            line, (grid[R_HI], 2, 8, ent_rows)
                        )
            agg = jnp.dot(hot_ref[rows, :], message_ref[:, cols], preferred_element_type=f32)
            agg = agg.reshape(2, grid[R_HI], 2, share, half)
            part_ref[step, :, :, :, :, cols] = agg
            part_sent[step, :, :, :, :, cols] = agg.astype(bf16)
            return carry

        lax.fori_loop(0, grid[E_HI], gather_sums, 0)
        if number == 0:
            pl.semaphore_wait(pltpu.get_barrier_semaphore(), greeted)
            counts.start()
        sums[number].start()

    for stage in range(4):
        counts.advance()
        sums[0].advance()
        sums[1].advance()
        if stage < 2:
            for step in range(2 * stage, 2 * stage + 2):
                rows = pl.ds(step * block, block)
                facts_t[:, rows] = jnp.transpose(facts_ref[rows, :])

    lane = lax.broadcasted_iota(jnp.int32, (share, ent_rows), 1)
    row = lax.broadcasted_iota(jnp.int32, (share, ent_rows), 0) + rep * share
    spread_counts = jnp.broadcast_to(counts.own[0:1, :], (share, ent_rows))
    count = jnp.sum(jnp.where(lane == row, spread_counts, 0.0), axis=1, keepdims=True)
    denom = jnp.maximum(count, 1.0)
    agg = jnp.concatenate([sums[0].own[...], sums[1].own[...]], axis=1)
    mean = (agg / denom).astype(bf16)
    zval = jnp.dot(mean, w_upd_ref[...], preferred_element_type=f32)
    grad_z = (cot_ref[rep].astype(f32) * silu_grad(zval)).astype(bf16)
    d_mean = lax.dot_general(
        grad_z, w_upd_ref[...], (((1,), (1,)), ((), ())), preferred_element_type=f32
    )
    all_ref[here] = (d_mean / denom).astype(bf16)
    for item in spreads:
        item.start()
    side = lax.dot_general(grad_z, mean, (((0,), (0,)), ((), ())), preferred_element_type=f32)
    side_ref[...] = side.reshape(side_ref.shape)
    side_sent[...] = side.astype(bf16).reshape(side_ref.shape)
    sides.start()
    ent_ref[rep] = (feats_ref[rep].astype(f32) + zval * jax.nn.sigmoid(zval)).astype(bf16)
    ent_copies = []
    for step in range(1, n_rep):
        copy = pltpu.make_async_remote_copy(
            src_ref=ent_ref.at[rep],
            dst_ref=ent_ref.at[rep],
            send_sem=ent_send.at[step - 1],
            recv_sem=ent_recv.at[step - 1],
            device_id={"rep": lax.rem(rep + step, n_rep)},
            device_id_type=MESH,
        )
        copy.start()
        ent_copies.append(copy)
    for stage in range(4):
        for item in spreads:
            item.advance()
    sides.advance()

    n_ents = ent_rows * grid[E_HI] * grid[E_LO]
    for number in range(2):

        def expand(step, carry):
            rows = pl.ds(pl.multiple_of(step * block, block), block)
            keys = jnp.concatenate([
                jnp.transpose(jnp.broadcast_to(
                    key_ref[:, pl.ds(pl.multiple_of(step * block + at, 128), 128)], (128, 128)
                ))
                for at in range(0, block, 128)
            ], axis=0)
            hits = jnp.concatenate([
                (keys == lax.broadcasted_iota(jnp.int32, (block, 128), 1) + at)
                .astype(f32).astype(bf16)
                for at in range(0, n_ents, 128)
            ], axis=1)
            d_msg = jnp.dot(
                hits, all_ref[...].reshape(n_ents, width), preferred_element_type=f32
            )
            d_pre_ref[rows, :] = (d_msg * gate_ref[rows, :]).astype(bf16)
            return carry

        lax.fori_loop(2 * number, 2 * number + 2, expand, 0)
        sides.advance()
    for number, cols in enumerate(halves):
        left = jnp.dot(facts_t[...], d_pre_ref[:, cols], preferred_element_type=f32)
        left = left.reshape(left_ref.shape[:-1] + (half,))
        left_ref[every + (cols,)] = left
        left_sent[every + (cols,)] = left.astype(bf16)
        lefts[number].start()
        if number == 0:
            sides.advance()
    for stage in range(4):
        for item in lefts:
            item.advance()
    for copy in ent_copies:
        copy.wait()
    grads_ref[:, 0:half] = lefts[0].own[...]
    grads_ref[:, half:width] = lefts[1].own[...]
    grads_ref[:, width:2 * width] = sides.own[...]


def in_vmem(number):
    return [pl.BlockSpec(memory_space=pltpu.VMEM)] * number


def per_device(facts, fact_owner, fact_slot, entity_feats, out_cotangent, w_msg, w_upd):
    n_owners = lax.axis_size("ent")
    n_copies = lax.axis_size("rep")
    grid = (n_owners // 2, 2, n_copies // 2, 2)
    fact_rows, width = facts.shape
    ent_rows = entity_feats.shape[0]
    ents = ent_rows * n_owners
    share = ent_rows // n_copies
    bf16, f32 = jnp.bfloat16, jnp.float32
    rows = width // (n_owners * n_copies)
    half = width // 2
    key = (fact_owner[:, 0] * ent_rows + fact_slot).reshape(1, fact_rows)
    hot_rows = ents if ents <= 1024 else 2 * ent_rows
    rep_sem = pltpu.SemaphoreType.DMA((n_copies - 1,))
    d_pre, ent_out, grads = pl.pallas_call(
        functools.partial(layer_kernel, grid),
        out_shape=(
            jax.ShapeDtypeStruct((fact_rows, width), bf16),
            jax.ShapeDtypeStruct((n_copies, share, width), bf16),
            jax.ShapeDtypeStruct((rows, 2 * width), f32),
        ),
        in_specs=in_vmem(6),
        out_specs=in_vmem(3),
        scratch_shapes=(
            [
                pltpu.VMEM((fact_rows, width), f32),
                pltpu.VMEM(grid + (share, width), f32),
                pltpu.VMEM(grid + (share, width), bf16),
                pltpu.VMEM((hot_rows, fact_rows), bf16),
                pltpu.VMEM((width, fact_rows), bf16),
                pltpu.VMEM(grid + (share, width), bf16),
                pltpu.VMEM(grid + (8, ent_rows), f32),
            ]
            + [
                pltpu.VMEM(grid + (rows, width), f32),
                pltpu.VMEM(grid + (rows, width), bf16),
            ] * 2
            + sum_scratch(grid, ORDER_A, (8, ent_rows), f32)
            + sum_scratch(grid, ORDER_A, (share, half), bf16)
            + sum_scratch(grid, ORDER_B, (share, half), bf16)
            + gather_scratch(grid, ORDER_A[::-1])
            + gather_scratch(grid, ORDER_B[::-1])
            + sum_scratch(grid, ORDER_A, (rows, width), bf16)
            + sum_scratch(grid, ORDER_A, (rows, half), bf16)
            + sum_scratch(grid, ORDER_B, (rows, half), bf16)
            + [rep_sem, rep_sem]
        ),
        compiler_params=pltpu.CompilerParams(
            collective_id=0, has_side_effects=True, vmem_limit_bytes=VMEM_LIMIT
        ),
    )(
        facts,
        key,
        entity_feats.reshape(n_copies, share, width),
        out_cotangent.reshape(n_copies, share, width),
        w_msg,
        w_upd,
    )
    fact_grad = lax.dot_general(
        d_pre, w_msg, (((1,), (1,)), ((), ())), preferred_element_type=f32
    ).astype(bf16)
    return (ent_out.reshape(ent_rows, width), fact_grad, grads[:, :width], grads[:, width:])


def solution(mesh):
    placed = (
        P(("ent", "rep"), None),
        P(("ent", "rep"), None),
        P(("ent", "rep")),
        P("ent", None),
        P("ent", None),
        P(),
        P(),
    )
    return jax.shard_map(
        per_device,
        mesh=mesh,
        in_specs=placed,
        out_specs=(
            P("ent", None),
            P(("ent", "rep"), None),
            P(("ent", "rep"), None),
            P(("ent", "rep"), None),
        ),
        check_vma=False,
    )
```

time: 80.7 us -> 75.3 us (0.933)
  Pallas kernels: 56.4 us -> 66 us
  matrix products: 13.7 us -> 4.23 us
  local copies, waits for them, and re-layouts: 7.03 us -> 2.07 us
    pallas_call x2 -> x1, Pallas kernels: 56.4 us -> 66 us  [per_device(): pl.pallas_call(functools.partial(layer_kernel, grid), out_shape=(jax.Shap...]
    dot_general x5 -> x1, matrix products: 13.7 us -> 4.23 us  [per_device(): lax.dot_general(d_pre, w_msg, (((1,), (1,)), ((), ())), preferred_element...]
    unnamed x18 -> x5, local copies, waits for them, and re-layouts: 6.27 us -> 0.67 us
    slice x0 -> x1, local copies, waits for them, and re-layouts: none -> 1.41 us  [per_device(): grads[:, width:]]
    reduce_sum x1 -> x0, other arithmetic: 0.91 us -> none  [per_device(): count = jnp.sum(onehot, axis=1, dtype=f32).reshape(grid + (1, share))]
where the time goes in v3:
time: 75.3 us; the launch traced here: 75 us
  Pallas kernels  66 us (88%)
  matrix products  4.23 us (6%)
  local copies, waits for them, and re-layouts  2.07 us (3%)
  other arithmetic  2.06 us (3%)
    pallas_call x1, Pallas kernels, per_device(): pl.pallas_call(functools.partial(layer_kernel, grid), out_shape=(jax.Shap...  66 us
    dot_general x1, matrix products, per_device(): lax.dot_general(d_pre, w_msg, (((1,), (1,)), ((), ())), preferred_element...  4.23 us

profile of v3, /device:TPU:0, one launch (start us, length us, event | category | flops | bytes accessed | tf_op | source)
XLA Modules:
  0.0 75.0 jit_solution(6020322626986226379)
XLA Ops:
  0.6 0.0 copy-start
  0.6 0.8 %broadcast_multiply_fusion = s32[2048,1]{0,1:T(1,128)S(1)} fusion(s32[2048,1]{0,1:T(1,128)} %param.8), kind=kLoop, calls=%fused_computation.1 | loop fusion | flops 2048 | bytes 16384 | tf_op jit(solution)/shard_map/mul | solution.py:341
  1.4 1.3 %add.3 = s32[2048]{0:T(1024)} add(s32[2048]{0:T(1024)S(1)} %bitcast.11, s32[2048]{0:T(1024)} %param.9) | non-fusion elementwise | flops 2048 | bytes 24576 | tf_op jit(solution)/shard_map/add | solution.py:341
  2.7 66.0 %shard_map.102 = (bf16[2048,512]{1,0:T(8,128)(2,1)}, bf16[4,32,512]{2,1,0:T(8,128)(2,1)}, f32[16,1024]{1,0:T(8,128)}) custom-call(bf16[2048,512]{1,0:T(8,128)(2,1)} %facts_ref.1, s32[1,2048]{1,0:T(1,128)} %bitcast.10, bf16[4,32,512]{2,1,0:T(8,128)(2,1)} %bitcast.8, bf16[4,32,512]{2,1,0:T(8,128)(2,1)} %bitcast.9, bf16[512,512]{1,0:T(8,128)(2,1)} %w_ref.1, ...), custom_call_target="tpu_custom_call" | custom-call | tf_op jit(solution)/shard_map/pallas_call | solution.py:344
  68.7 1.4 %fusion = (f32[16,512]{1,0:T(8,128)}, f32[16,512]{1,0:T(8,128)}) fusion(f32[16,1024]{1,0:T(8,128)} %get-tuple-element.9), kind=kLoop, calls=%fused_computation.2 | loop fusion | bytes 131072 | tf_op jit(solution)/shard_map/slice | solution.py:391
  70.1 0.0 copy-done
  70.1 0.0 copy-start.1
  70.1 4.2 %convolution_convert_fusion = bf16[2048,512]{1,0:T(8,128)(2,1)} fusion(bf16[2048,512]{1,0:T(8,128)(2,1)} %get-tuple-element.8, bf16[512,512]{1,0:T(8,128)(2,1)S(1)} %copy-done), kind=kOutput, calls=%fused_computation | convolution fusion | flops 1074790400 | bytes 4718592 | tf_op jit(solution)/shard_map/dot_general | solution.py:388
  74.3 0.0 copy-done.1
  74.3 0.7 copy.12
Async XLA Ops:
  0.6 69.5 %copy-start = (bf16[512,512]{1,0:T(8,128)(2,1)S(1)}, bf16[512,512]{1,0:T(8,128)(2,1)}, u32[]{:S(2)}) copy-start(bf16[512,512]{1,0:T(8,128)(2,1)} %w_ref.1) | copy-start | bytes 1572868
  70.1 4.2 %copy-start.1 = (bf16[4,32,512]{2,1,0:T(8,128)(2,1)S(1)}, bf16[4,32,512]{2,1,0:T(8,128)(2,1)}, u32[]{:S(2)}) copy-start(bf16[4,32,512]{2,1,0:T(8,128)(2,1)} %get-tuple-element.7) | copy-start | bytes 393220

commit v4 on v3

--- a/solution.py
+++ b/solution.py
@@ -11,7 +11,7 @@
 ORDER_A = (R_LO, R_HI, E_LO, E_HI)
 ORDER_B = (R_LO, E_LO, R_HI, E_HI)
 MESH = pl.DeviceIdType.MESH
-VMEM_LIMIT = 56 << 20
+VMEM_LIMIT = 60 << 20
 
 
 def silu_grad(value):
@@ -152,8 +152,8 @@
     return [pltpu.SemaphoreType.DMA((grid[d] - 1,)) for d in order for _ in range(2)]
 
 
-def layer_kernel(grid, facts_ref, key_ref, feats_ref, cot_ref, w_ref, w_upd_ref,
-                 d_pre_ref, ent_ref, grads_ref, *scratch):
+def layer_kernel(grid, facts_ref, owner_ref, slot_ref, feats_ref, cot_ref, w_ref, w_upd_ref,
+                 fact_ref, ent_ref, msg_ref, upd_ref, *scratch):
     bf16, f32 = jnp.bfloat16, jnp.float32
     here = position()
     rep = lax.axis_index("rep")
@@ -167,6 +167,7 @@
 
     gate_ref, part_ref, part_sent, hot_ref, facts_t, all_ref, count_ref = take(7)
     side_ref, side_sent, left_ref, left_sent = take(4)
+    d_pre_ref, key_ref, hits_ref = take(3)
     message_ref = d_pre_ref
     fact_rows, width = facts_ref.shape
     half = width // 2
@@ -176,6 +177,8 @@
     block = fact_rows // 4
     pair = 2 * ent_rows
     kept = hot_ref.shape[0] > pair
+    n_ents = ent_rows * grid[E_HI] * grid[E_LO]
+    key_ref[...] = owner_ref[...] * ent_rows + slot_ref[...]
     every = (slice(None),) * 5
     counts = Scatter(grid, here, ORDER_A, count_ref, count_ref, take(20))
     sums = [
@@ -276,34 +279,43 @@
         )
         copy.start()
         ent_copies.append(copy)
+
+    piece = block if kept else block // 4
+    pieces = fact_rows // piece
+
+    def build_hits(step):
+        keys = jnp.concatenate([
+            jnp.transpose(jnp.broadcast_to(
+                key_ref[:, pl.ds(pl.multiple_of(step * piece + at, 128), 128)], (128, 128)
+            ))
+            for at in range(0, piece, 128)
+        ], axis=0)
+        place = pl.ds(pl.multiple_of(step * piece, piece), piece) if kept else pl.ds(0, piece)
+        for at in range(0, n_ents, 128):
+            ids = lax.broadcasted_iota(jnp.int32, (piece, 128), 1) + at
+            hits_ref[place, at:at + 128] = (keys == ids).astype(f32).astype(bf16)
+
     for stage in range(4):
+        if kept:
+            build_hits(stage)
         for item in spreads:
             item.advance()
     sides.advance()
 
-    n_ents = ent_rows * grid[E_HI] * grid[E_LO]
     for number in range(2):
 
         def expand(step, carry):
-            rows = pl.ds(pl.multiple_of(step * block, block), block)
-            keys = jnp.concatenate([
-                jnp.transpose(jnp.broadcast_to(
-                    key_ref[:, pl.ds(pl.multiple_of(step * block + at, 128), 128)], (128, 128)
-                ))
-                for at in range(0, block, 128)
-            ], axis=0)
-            hits = jnp.concatenate([
-                (keys == lax.broadcasted_iota(jnp.int32, (block, 128), 1) + at)
-                .astype(f32).astype(bf16)
-                for at in range(0, n_ents, 128)
-            ], axis=1)
+            rows = pl.ds(pl.multiple_of(step * piece, piece), piece)
+            if not kept:
+                build_hits(step)
+            hits = hits_ref[rows if kept else pl.ds(0, piece), :]
             d_msg = jnp.dot(
                 hits, all_ref[...].reshape(n_ents, width), preferred_element_type=f32
             )
             d_pre_ref[rows, :] = (d_msg * gate_ref[rows, :]).astype(bf16)
             return carry
 
-        lax.fori_loop(2 * number, 2 * number + 2, expand, 0)
+        lax.fori_loop(number * pieces // 2, (number + 1) * pieces // 2, expand, 0)
         sides.advance()
     for number, cols in enumerate(halves):
         left = jnp.dot(facts_t[...], d_pre_ref[:, cols], preferred_element_type=f32)
@@ -314,13 +326,36 @@
         if number == 0:
             sides.advance()
     for stage in range(4):
+        rows = pl.ds(stage * block, block)
+        fact_ref[rows, :] = lax.dot_general(
+            d_pre_ref[rows, :], w_ref[...], (((1,), (1,)), ((), ())), preferred_element_type=f32
+        ).astype(bf16)
         for item in lefts:
             item.advance()
     for copy in ent_copies:
         copy.wait()
-    grads_ref[:, 0:half] = lefts[0].own[...]
-    grads_ref[:, half:width] = lefts[1].own[...]
-    grads_ref[:, width:2 * width] = sides.own[...]
+    msg_ref[:, 0:half] = lefts[0].own[...]
+    msg_ref[:, half:width] = lefts[1].own[...]
+    upd_ref[...] = sides.own[...]
+
+
+def hand_over_kernel(*refs):
+    number = (len(refs) - 1) // 2
+    sems = refs[-1]
+    copies = []
+    for index in range(number):
+        source, target = refs[index], refs[number + index]
+        parts = 4 if index == 0 else 1
+        rows = source.shape[0] // parts
+        for part in range(parts):
+            place = pl.ds(part * rows, rows)
+            copy = pltpu.make_async_copy(
+                source.at[place], target.at[place], sems.at[len(copies)]
+            )
+            copy.start()
+            copies.append(copy)
+    for copy in copies:
+        copy.wait()
 
 
 def in_vmem(number):
@@ -338,18 +373,18 @@
     bf16, f32 = jnp.bfloat16, jnp.float32
     rows = width // (n_owners * n_copies)
     half = width // 2
-    key = (fact_owner[:, 0] * ent_rows + fact_slot).reshape(1, fact_rows)
     hot_rows = ents if ents <= 1024 else 2 * ent_rows
     rep_sem = pltpu.SemaphoreType.DMA((n_copies - 1,))
-    d_pre, ent_out, grads = pl.pallas_call(
+    results = pl.pallas_call(
         functools.partial(layer_kernel, grid),
         out_shape=(
             jax.ShapeDtypeStruct((fact_rows, width), bf16),
             jax.ShapeDtypeStruct((n_copies, share, width), bf16),
-            jax.ShapeDtypeStruct((rows, 2 * width), f32),
+            jax.ShapeDtypeStruct((rows, width), f32),
+            jax.ShapeDtypeStruct((rows, width), f32),
         ),
-        in_specs=in_vmem(6),
-        out_specs=in_vmem(3),
+        in_specs=in_vmem(7),
+        out_specs=in_vmem(4),
         scratch_shapes=(
             [
                 pltpu.VMEM((fact_rows, width), f32),
@@ -364,6 +399,11 @@
                 pltpu.VMEM(grid + (rows, width), f32),
                 pltpu.VMEM(grid + (rows, width), bf16),
             ] * 2
+            + [
+                pltpu.VMEM((fact_rows, width), bf16),
+                pltpu.VMEM((1, fact_rows), jnp.int32),
+                pltpu.VMEM((fact_rows if ents <= 1024 else fact_rows // 16, ents), bf16),
+            ]
             + sum_scratch(grid, ORDER_A, (8, ent_rows), f32)
             + sum_scratch(grid, ORDER_A, (share, half), bf16)
             + sum_scratch(grid, ORDER_B, (share, half), bf16)
@@ -379,16 +419,21 @@
         ),
     )(
         facts,
-        key,
+        fact_owner.reshape(1, fact_rows),
+        fact_slot.reshape(1, fact_rows),
         entity_feats.reshape(n_copies, share, width),
         out_cotangent.reshape(n_copies, share, width),
         w_msg,
         w_upd,
     )
-    fact_grad = lax.dot_general(
-        d_pre, w_msg, (((1,), (1,)), ((), ())), preferred_element_type=f32
-    ).astype(bf16)
-    return (ent_out.reshape(ent_rows, width), fact_grad, grads[:, :width], grads[:, width:])
+    fact_grad, ent_out, msg_grad, upd_grad = pl.pallas_call(
+        hand_over_kernel,
+        out_shape=tuple(jax.ShapeDtypeStruct(item.shape, item.dtype) for item in results),
+        in_specs=[pl.BlockSpec(memory_space=pl.ANY)] * 4,
+        out_specs=tuple([pl.BlockSpec(memory_space=pl.ANY)] * 4),
+        scratch_shapes=[pltpu.SemaphoreType.DMA((7,))],
+    )(*results)
+    return (ent_out.reshape(ent_rows, width), fact_grad, msg_grad, upd_grad)
 
 
 def solution(mesh):

time: 75.3 us -> 138 us (1.83)
  Pallas kernels: 66 us -> 137 us
  matrix products: 4.23 us -> 0 us
  local copies, waits for them, and re-layouts: 2.07 us -> 0 us
  other arithmetic: 2.06 us -> 0 us
    pallas_call x0 -> x1, Pallas kernels: none -> 70.7 us  [per_device(): pl.pallas_call(hand_over_kernel, out_shape=tuple((jax.ShapeDtypeStruct(it...]
    dot_general x1 -> x0, matrix products: 4.23 us -> none  [per_device(): lax.dot_general(d_pre, w_msg, (((1,), (1,)), ((), ())), preferred_element...]
    slice x1 -> x0, local copies, waits for them, and re-layouts: 1.41 us -> none  [per_device(): grads[:, width:]]
where the time goes in v4:
time: 138 us
  Pallas kernels  137 us (99%)
    pallas_call x1, Pallas kernels, per_device(): pl.pallas_call(hand_over_kernel, out_shape=tuple((jax.ShapeDtypeStruct(it...  70.7 us
    pallas_call x1, Pallas kernels, per_device(): pl.pallas_call(functools.partial(layer_kernel, grid), out_shape=(jax.Shap...  66.4 us

profile of v4, /device:TPU:0, one launch (start us, length us, event | category | flops | bytes accessed | tf_op | source)
XLA Modules:
  0.0 137.7 jit_solution(13626499426499716823)
XLA Ops:
  0.6 66.4 %shard_map.102 = (bf16[2048,512]{1,0:T(8,128)(2,1)}, bf16[4,32,512]{2,1,0:T(8,128)(2,1)}, f32[16,512]{1,0:T(8,128)}, f32[16,512]{1,0:T(8,128)}) custom-call(bf16[2048,512]{1,0:T(8,128)(2,1)} %facts_ref.1, s32[1,2048]{1,0:T(1,128)} %bitcast.7, s32[1,2048]{1,0:T(1,128)} %bitcast.8, bf16[4,32,512]{2,1,0:T(8,128)(2,1)} %bitcast.5, bf16[4,32,512]{2,1,0:T(8,128)(2,1)} %bitcast.6, ...), custom_call_target="tpu_custom_call" | custom-call | tf_op jit(solution)/shard_map/pallas_call | solution.py:378
  67.1 70.7 %shard_map.103 = (bf16[2048,512]{1,0:T(8,128)(2,1)}, bf16[4,32,512]{2,1,0:T(8,128)(2,1)}, f32[16,512]{1,0:T(8,128)}, f32[16,512]{1,0:T(8,128)}) custom-call(bf16[2048,512]{1,0:T(8,128)(2,1)} %get-tuple-element.12.refs_0_, bf16[4,32,512]{2,1,0:T(8,128)(2,1)} %get-tuple-element.13.refs_1_, f32[16,512]{1,0:T(8,128)} %get-tuple-element.14.refs_2_, ...), custom_call_target="tpu_custom_call" | custom-call | tf_op jit(solution)/shard_map/pallas_call | solution.py:429
